TPU v7x, 256 devices: a whole 4x4x8 slice. The times are simulated.
256 devices in a mesh: hist: 4 (over x), ka: 64 (over z, y, core).
Axes of the slice: x: 4, y: 4, z: 8, core: 2. Of those that a mesh axis runs over, the one named last changes fastest.
Arguments:
- g_row: float32 [2, 16, 128, 1024], P(None, None, None, 'ka'), may hold values from -6 to 6
- w_row: float32 [2, 16, 128, 1024], P(None, None, None, 'ka'), may hold values from -192 to 192
- g_hist: bfloat16 [2, 16, 1024, 128, 128], P(None, None, 'ka', 'hist'), may hold values from -6 to 6
- s_hist: bfloat16 [2, 16, 1024, 128, 128], P(None, None, 'ka', 'hist'), may hold values from -6 to 6
- step_now: int32 [1], replicated, may hold values from 64 to 128
Outputs:
- memory_integral: float32 [2, 16, 1024, 128], P(None, None, 'ka', 'hist')
All inputs are finite; a program needn't handle non-finite values.
Results may differ from a plain program's by a relative error of at most 0.0029.
Values may be sent and summed in bfloat16 or wider, within the bound.
A program may use at most 128 MiB of HBM per device.

v0:
```python
import functools
import math

import jax
import jax.numpy as jnp
import ml_dtypes
import numpy as np
from jax import lax
from jax.experimental import pallas as pl
from jax.experimental.pallas import tpu as pltpu
from jax.sharding import PartitionSpec as P

LX = 32
NORB = 4
PAIRS = 16
MESH = pl.DeviceIdType.MESH
F32 = jnp.float32
BF16 = jnp.bfloat16


def split_table(table):
    high = table.astype(ml_dtypes.bfloat16)
    low = (table - high.astype(np.float64)).astype(ml_dtypes.bfloat16)
    return high, low


def tables():
    step = np.arange(LX)
    theta = 2.0 * math.pi * (step[:, None] * step[None, :] % LX) / LX
    cosine, sine = np.cos(theta), np.sin(theta)
    first = np.block([[cosine, sine], [-sine, cosine]])
    high, low = split_table(first)
    first = np.concatenate([high, low, high], axis=1)
    last = np.stack(
        [np.concatenate([-sine, -cosine], 1), np.concatenate([cosine, -sine], 1)],
        axis=1,
    ).reshape(2 * LX, 2 * LX) / float(LX**4)
    high, low = split_table(last)
    last = np.concatenate([high, low, high], axis=1)
    eye = np.eye(8)

    def along(table):
        cut = table.reshape(2, 16, LX)
        return np.einsum("hky,pq->hpkqy", cut, eye).reshape(256, 256)

    forth = np.concatenate([along(cosine), along(sine)], axis=1)
    back = np.concatenate([along(cosine).T, along(sine).T], axis=1)
    return (first, last) + split_table(forth) + split_table(back)


def cut(value):
    high = value.astype(BF16)
    low = (value - high.astype(F32)).astype(BF16)
    return high, low


def dot(left, right):
    return jnp.dot(left, right, preferred_element_type=F32)


def fine_dot(left, right_high, right_low):
    rows = left.shape[0]
    high, low = cut(left)
    both = dot(jnp.concatenate([high, low], axis=0), right_high)
    return both[:rows] + both[rows:] + dot(high, right_low)


def four(i):
    return pl.ds(pl.multiple_of(4 * i, 4), 4)


def convolve(block, first, last, forth, back):
    data = jnp.concatenate(
        [
            jnp.concatenate([block(a, 0, half), block(a, 1, half)], axis=0)
            for a in range(2)
            for half in range(2)
        ],
        axis=1,
    )
    high, low = cut(data)
    stage = dot(first, jnp.concatenate([high, high, low], axis=0))
    stage = jnp.concatenate([stage[:, :256], stage[:, 256:]], axis=0)
    stage = fine_dot(stage, *forth)
    parts = []
    for a in range(2):
        re, im = stage[64 * a : 64 * a + 32], stage[64 * a + 32 : 64 * a + 64]
        parts.append((re[:, :256] + im[:, 256:], im[:, :256] - re[:, 256:]))
    (g_re, g_im), (w_re, w_im) = parts
    prod = jnp.concatenate([g_re * w_re - g_im * w_im, g_re * w_im + g_im * w_re], axis=0)
    stage = fine_dot(prod, *back)
    re, im = stage[:32], stage[32:]
    stage = jnp.concatenate([re[:, :256] - im[:, 256:], im[:, :256] + re[:, 256:]], axis=0)
    high, low = cut(stage)
    return dot(last, jnp.concatenate([high, high, low], axis=0))


def kernel(
    n_ka, n_hist,
    step_ref, g_hbm, w_hbm, gh_hbm, sh_hbm, first_hbm, last_hbm, fh_hbm, fl_hbm, bh_hbm, bl_hbm,
    out_ref,
    rows_v, gh_v, sh_v, first_v, last_v, fh_v, fl_v, bh_v, bl_v,
    turned, send_rows, recv_rows, send_sig, recv_sig, wide_sig, left_g, left_s, partial, rs_send, rs_recv, summed,
    row_sem, table_sem, sh_sem, gh_sem, self_sem, send_sem, recv_sem,
):
    hist = lax.axis_index("hist")
    me = lax.axis_index("ka")
    slab = LX

    row_copies = [
        pltpu.make_async_copy(g_hbm, rows_v.at[0], row_sem.at[0]),
        pltpu.make_async_copy(w_hbm, rows_v.at[1], row_sem.at[1]),
    ]
    for copy in row_copies:
        copy.start()

    barrier = pltpu.get_barrier_semaphore()

    def greet(i, carry):
        pl.semaphore_signal(barrier, inc=1, device_id={"ka": lax.rem(me + i, n_ka)}, device_id_type=MESH)
        return carry

    lax.fori_loop(1, n_ka, greet, 0)
    for d in range(1, n_hist):
        pl.semaphore_signal(barrier, inc=1, device_id={"hist": lax.rem(hist + d, n_hist)}, device_id_type=MESH)

    table_copies = [
        pltpu.make_async_copy(src, dst, table_sem.at[i])
        for i, (src, dst) in enumerate(
            [(first_hbm, first_v), (last_hbm, last_v), (fh_hbm, fh_v), (fl_hbm, fl_v), (bh_hbm, bh_v), (bl_hbm, bl_v)]
        )
    ]
    chunks = 4
    width = 16 // chunks
    sh_copies = [
        pltpu.make_async_copy(
            sh_hbm.at[:, :, pl.ds(q * width, width)], sh_v.at[:, :, pl.ds(q * width, width)], sh_sem.at[q]
        )
        for q in range(chunks)
    ]
    gh_copies = [
        pltpu.make_async_copy(
            gh_hbm.at[:, :, pl.ds(q * width, width)], gh_v.at[:, :, pl.ds(q * width, width)], gh_sem.at[q]
        )
        for q in range(chunks)
    ]
    for copy in table_copies + sh_copies + gh_copies:
        copy.start()

    for copy in row_copies:
        copy.wait()
    for a in range(2):
        for part in range(2):
            r = 2 * a + part
            for ph in range(2):
                turned[2 * r + ph] = rows_v[a, part, pl.ds(128 * ph, 128), :].T
    for r in range(4):
        for ph in range(2):
            send_rows[pl.ds(4 * ph + r, 32, stride=8), :] = turned[2 * r + ph, pl.ds(slab * hist, slab), :]

    pl.semaphore_wait(barrier, n_ka - 1 + n_hist - 1)

    def send_row(i, carry):
        to = lax.rem(me + i, n_ka)
        pltpu.make_async_remote_copy(
            src_ref=send_rows.at[four(to)], dst_ref=recv_rows.at[four(me)], send_sem=send_sem.at[0], recv_sem=recv_sem.at[0],
            device_id={"ka": to}, device_id_type=MESH,
        ).start()
        return carry

    lax.fori_loop(1, n_ka, send_row, 0)
    own_row = pltpu.make_async_copy(send_rows.at[four(me)], recv_rows.at[four(me)], self_sem.at[0])
    own_row.start()

    lane = lax.broadcasted_iota(jnp.int32, (1, 128), 1)
    place = lane // 32
    alive = (hist * slab + lane % 32) < step_ref[0]

    def spread(left, pieces):
        for part in range(2):
            for a in range(NORB):
                row = pieces(part, a, 0)
                for b in range(1, NORB):
                    row = jnp.where(place == b, pieces(part, a, b), row)
                row = jnp.where(alive, row, 0.0)
                if part == 0:
                    left[0, pl.ds(a, 16, stride=8), :] = row
                    left[1, pl.ds(4 + a, 16, stride=8), :] = row
                else:
                    left[1, pl.ds(a, 16, stride=8), :] = -row
                    left[0, pl.ds(4 + a, 16, stride=8), :] = row

    def green_piece(part, a, b):
        block = rows_v[0, part, pl.ds((4 * a + b) * 16, 16), :]
        return pltpu.roll(block, lax.rem(32 * b + 128 - 32 * hist, 128), 1)

    spread(left_g, green_piece)

    def left_of(left, k):
        at = pl.ds(8 * k, 8)
        return jnp.concatenate([left[0, at, :], left[1, at, :]], axis=1).astype(BF16)

    s_at = lax.broadcasted_iota(jnp.int32, (slab, 128), 0) + hist * slab
    t_at = lax.broadcasted_iota(jnp.int32, (slab, 128), 1)
    lower = jnp.where(s_at >= t_at, 1.0, 0.0).astype(BF16)

    def history(ref, k):
        return jnp.concatenate(
            [
                jnp.concatenate(
                    [ref[part, 4 * b + c, k] * lower for part in range(2) for b in range(NORB)], axis=0
                )
                for c in range(NORB)
            ],
            axis=1,
        )

    for q in range(chunks):
        sh_copies[q].wait()
        for kk in range(width):
            k = q * width + kk
            partial[k] = dot(left_of(left_g, k), history(sh_v, k))

    for copy in table_copies:
        copy.wait()
    own_row.wait()
    rest = recv_rows.at[pl.ds(0, 4 * (n_ka - 1))]
    pltpu.make_async_copy(rest, rest, recv_sem.at[0]).wait()

    def block(a, part, half):
        return recv_rows[pl.ds(4 * half + 2 * a + part, 32, stride=8), :]

    sigma = convolve(block, first_v[...], last_v[...], (fh_v[...], fl_v[...]), (bh_v[...], bl_v[...])).astype(BF16)
    for half in range(2):
        send_sig[half] = sigma[:, 128 * half : 128 * half + 128].reshape(LX, 2, 128)

    time, group = me // 2, lax.rem(me, 2)
    landing = group * LX + time

    def send_sigma(i, carry):
        to = lax.rem(me + i, n_ka)
        pltpu.make_async_remote_copy(
            src_ref=send_sig.at[lax.rem(to, 2), to // 2], dst_ref=recv_sig.at[landing],
            send_sem=send_sem.at[1], recv_sem=recv_sem.at[1], device_id={"ka": to}, device_id_type=MESH,
        ).start()
        return carry

    lax.fori_loop(1, n_ka, send_sigma, 0)
    own_sig = pltpu.make_async_copy(send_sig.at[group, time], recv_sig.at[landing], self_sem.at[1])
    own_sig.start()
    own_sig.wait()
    most = recv_sig.at[pl.ds(0, n_ka - 1)]
    pltpu.make_async_copy(most, most, recv_sem.at[1]).wait()

    wide_sig[...] = recv_sig[...].reshape(2, 2 * LX, 128).astype(F32)
    stacked = jnp.concatenate(
        [wide_sig[ph, pl.ds(part, 32, stride=2), :] for part in range(2) for ph in range(2)], axis=0
    ).T

    def sigma_piece(part, a, b):
        ph = a // 2
        at = ((a % 2) * 4 + b) * 16
        shift = (32 * (b - 2 * part - ph)) % 128
        rows = stacked[at : at + 16]
        return pltpu.roll(rows, shift, 1) if shift else rows

    spread(left_s, sigma_piece)

    for q in range(chunks):
        gh_copies[q].wait()
        for kk in range(width):
            k = q * width + kk
            total = partial[k] + dot(left_of(left_s, k), history(gh_v, k))
            columns = [total[:, 128 * c : 128 * c + 128] for c in range(NORB)]
            for to in range(NORB):
                row = None
                for c in range(NORB):
                    shift = (32 * (c - to)) % 128
                    moved = pltpu.roll(columns[c], shift, 1) if shift else columns[c]
                    row = moved if row is None else jnp.where(place == c, moved, row)
                rs_send[to, k] = row
        for d in range(1, n_hist):
            to = lax.rem(hist + d, n_hist)
            pltpu.make_async_remote_copy(
                src_ref=rs_send.at[to, pl.ds(q * width, width)],
                dst_ref=rs_recv.at[n_hist - 1 - d, pl.ds(q * width, width)],
                send_sem=send_sem.at[2], recv_sem=recv_sem.at[2], device_id={"hist": to}, device_id_type=MESH,
            ).start()

    pltpu.make_async_copy(rs_recv, rs_recv, recv_sem.at[2]).wait()
    scale = 2.0 / (n_hist * slab)
    summed[...] = ((rs_recv[0] + rs_recv[1]) + (rs_recv[2] + rs_send[hist])).reshape(128, 128) * scale
    for m in range(8):
        rows = summed[pl.ds(m, 16, stride=8), :]
        for c in range(NORB):
            moved = pltpu.roll(rows, 128 - 32 * c, 1) if c else rows
            out_ref[m // 4, (m % 4) * 4 + c] = moved[:, :slab]

    pltpu.make_async_copy(rest, rest, send_sem.at[0]).wait()
    pltpu.make_async_copy(most, most, send_sem.at[1]).wait()
    pltpu.make_async_copy(rs_recv, rs_recv, send_sem.at[2]).wait()


def per_device(n_ka, n_hist, g_row, w_row, g_hist, s_hist, step_now):
    rows = [jnp.transpose(x, (0, 1, 3, 2)).reshape(2, PAIRS * 16, 128) for x in (g_row, w_row)]
    first, last, fh, fl, bh, bl = (jnp.asarray(t) for t in tables())
    anywhere = pl.BlockSpec(memory_space=pltpu.HBM)
    return pl.pallas_call(
        functools.partial(kernel, n_ka, n_hist),
        out_shape=jax.ShapeDtypeStruct((2, PAIRS, 16, 32), F32),
        in_specs=[pl.BlockSpec(memory_space=pltpu.SMEM)] + [anywhere] * 10,
        out_specs=pl.BlockSpec(memory_space=pltpu.VMEM),
        scratch_shapes=[
            pltpu.VMEM((2, 2, 256, 128), F32),
            pltpu.VMEM((2, 16, 16, 32, 128), BF16),
            pltpu.VMEM((2, 16, 16, 32, 128), BF16),
            pltpu.VMEM((64, 192), BF16),
            pltpu.VMEM((64, 192), BF16),
            pltpu.VMEM((256, 512), BF16),
            pltpu.VMEM((256, 512), BF16),
            pltpu.VMEM((256, 512), BF16),
            pltpu.VMEM((256, 512), BF16),
            pltpu.VMEM((8, 128, 128), F32),
            pltpu.VMEM((256, 128), F32),
            pltpu.VMEM((256, 128), F32),
            pltpu.VMEM((2, 32, 2, 128), BF16),
            pltpu.VMEM((64, 2, 128), BF16),
            pltpu.VMEM((2, 64, 128), F32),
            pltpu.VMEM((2, 128, 128), F32),
            pltpu.VMEM((2, 128, 128), F32),
            pltpu.VMEM((16, 8, 512), F32),
            pltpu.VMEM((4, 16, 8, 128), F32),
            pltpu.VMEM((3, 16, 8, 128), F32),
            pltpu.VMEM((128, 128), F32),
            pltpu.SemaphoreType.DMA((2,)),
            pltpu.SemaphoreType.DMA((6,)),
            pltpu.SemaphoreType.DMA((4,)),
            pltpu.SemaphoreType.DMA((4,)),
            pltpu.SemaphoreType.DMA((2,)),
            pltpu.SemaphoreType.DMA((3,)),
            pltpu.SemaphoreType.DMA((3,)),
        ],
        compiler_params=pltpu.CompilerParams(
            collective_id=0, has_side_effects=True, vmem_limit_bytes=60 * 1024 * 1024
        ),
    )(step_now, *rows, g_hist, s_hist, first, last, fh, fl, bh, bl)


def solution(mesh):
    placed = (
        P(None, None, None, "ka"),
        P(None, None, None, "ka"),
        P(None, None, "ka", "hist", None),
        P(None, None, "ka", "hist", None),
        P(),
    )
    return jax.shard_map(
        functools.partial(per_device, mesh.shape["ka"], mesh.shape["hist"]),
        mesh=mesh,
        in_specs=placed,
        out_specs=P(None, None, "ka", "hist"),
        check_vma=False,
    )
```

profile of v0, /device:TPU:1, one launch (start us, length us, event | category | flops | bytes accessed | tf_op | source)
XLA Modules:
  0.0 36.1 jit_solution(7469465449677533353)
XLA Ops:
  0.7 33.7 %shard_map.109 = f32[2,16,16,32]{3,2,1,0:T(8,128)} custom-call(s32[1]{0:T(128)S(6)} %copy.13.step_ref, f32[2,256,128]{2,1,0:T(8,128)} %bitcast.6, f32[2,256,128]{2,1,0:T(8,128)} %bitcast.7, bf16[2,16,16,32,128]{4,3,2,1,0:T(8,128)(2,1)} %gh_hbm.1, bf16[2,16,16,32,128]{4,3,2,1,0:T(8,128)(2,1)} %sh_hbm.1, bf16[64,192]{1,0:T(8,128)(2,1)} %constant.12.clone.first_hbm, ...), custom_call_target="tpu_custom_call" | custom-call | tf_op jit(solution)/shard_map/pallas_call | solution.py:308
  34.4 1.7 %copy.14 = f32[2,16,16,32]{3,2,1,0:T(8,128)} copy(f32[2,16,16,32]{3,2,1,0:T(8,128)} %shard_map.109) | data formatting | bytes 131072
where the time goes:
time: 36.2 us; the launch traced here: 36.1 us
  Pallas kernels  33.7 us (93%)
  local copies, waits for them, and re-layouts  1.67 us (5%)
  between operations  0.66 us (2%)
    pallas_call x1, Pallas kernels, per_device(): pl.pallas_call(functools.partial(kernel, n_ka, n_hist), out_shape=jax.Sha...  33.7 us
    unnamed x1, local copies, waits for them, and re-layouts  1.67 us

commit v1 on v0

v1 whole, which is shorter than its diff:
```python
import functools
import math

import jax
import jax.numpy as jnp
import ml_dtypes
import numpy as np
from jax import lax
from jax.experimental import pallas as pl
from jax.experimental.pallas import tpu as pltpu
from jax.sharding import PartitionSpec as P

LX = 32
NORB = 4
LIMIT = 54800
PAIRS = 16
MESH = pl.DeviceIdType.MESH
F32 = jnp.float32
BF16 = jnp.bfloat16


def split_table(table):
    high = table.astype(ml_dtypes.bfloat16)
    low = (table - high.astype(np.float64)).astype(ml_dtypes.bfloat16)
    return high, low


def tables():
    step = np.arange(LX)
    theta = 2.0 * math.pi * (step[:, None] * step[None, :] % LX) / LX
    cosine, sine = np.cos(theta), np.sin(theta)
    first = np.block([[cosine, sine], [-sine, cosine]])
    high, low = split_table(first)
    first = np.concatenate([high, low, high], axis=1)
    last = np.stack(
        [np.concatenate([-sine, -cosine], 1), np.concatenate([cosine, -sine], 1)],
        axis=1,
    ).reshape(2 * LX, 2 * LX) / float(LX**4)
    high, low = split_table(last)
    last = np.concatenate([high, low, high], axis=1)
    eye = np.eye(8)

    def along(table):
        cut = table.reshape(2, 16, LX)
        return np.einsum("hky,pq->hpkqy", cut, eye).reshape(256, 256)

    forth = np.concatenate([along(cosine), along(sine)], axis=1)
    back = np.concatenate([along(cosine).T, along(sine).T], axis=1)
    ends = np.zeros((128, 512), ml_dtypes.bfloat16)
    ends[:64, :192], ends[64:, :192] = first, last
    return np.concatenate(split_table(forth) + split_table(back) + (ends,), axis=0)


def cut(value):
    high = value.astype(BF16)
    low = (value - high.astype(F32)).astype(BF16)
    return high, low


def dot(left, right):
    return jnp.dot(left, right, preferred_element_type=F32)


def fine_dot(left, right_high, right_low):
    rows = left.shape[0]
    high, low = cut(left)
    both = dot(jnp.concatenate([high, low], axis=0), right_high)
    return both[:rows] + both[rows:] + dot(high, right_low)


def convolve(block, table):
    first, last = table[1024:1088, :192], table[1088:1152, :192]
    forth = table[0:256, :], table[256:512, :]
    back = table[512:768, :], table[768:1024, :]
    data = jnp.concatenate(
        [
            jnp.concatenate([block(ph, a, 0, half), block(ph, a, 1, half)], axis=0)
            for ph in range(2)
            for a in range(2)
            for half in range(2)
        ],
        axis=1,
    )
    high, low = cut(data)
    stage = dot(first, jnp.concatenate([high, high, low], axis=0))
    stage = jnp.concatenate([stage[:, 256 * i : 256 * i + 256] for i in range(4)], axis=0)
    stage = fine_dot(stage, *forth)
    prods = []
    for ph in range(2):
        parts = []
        for i in (2 * ph, 2 * ph + 1):
            re, im = stage[64 * i : 64 * i + 32], stage[64 * i + 32 : 64 * i + 64]
            parts.append((re[:, :256] + im[:, 256:], im[:, :256] - re[:, 256:]))
        (g_re, g_im), (w_re, w_im) = parts
        prods += [g_re * w_re - g_im * w_im, g_re * w_im + g_im * w_re]
    stage = fine_dot(jnp.concatenate(prods, axis=0), *back)
    wide = []
    for ph in range(2):
        re, im = stage[64 * ph : 64 * ph + 32], stage[64 * ph + 32 : 64 * ph + 64]
        wide.append(jnp.concatenate([re[:, :256] - im[:, 256:], im[:, :256] + re[:, 256:]], axis=0))
    high, low = cut(jnp.concatenate(wide, axis=1))
    return dot(last, jnp.concatenate([high, high, low], axis=0))


def kernel(
    n_ka, n_hist,
    step_hbm, g_hbm, w_hbm, gh_hbm, sh_hbm, table_hbm,
    out_ref,
    step_ref, rows_v, gh_v, sh_v, table_v,
    turned, send_rows, recv_rows, send_sig, recv_sig, wide_sig, left_g, left_s, partial, rs_full, rs_send, rs_recv, summed,
    row_sem, table_sem, sh_sem, gh_sem, self_sem, send_sem, recv_sem,
):
    hist = lax.axis_index("hist")
    me = lax.axis_index("ka")
    slab = LX
    n_conv = slab
    convolver = me < n_conv
    barrier = pltpu.get_barrier_semaphore()

    row_copies = [
        pltpu.make_async_copy(src.at[part], rows_v.at[a, part], row_sem.at[a, part])
        for a, src in enumerate((g_hbm, w_hbm))
        for part in range(2)
    ]
    for copy in row_copies:
        copy.start()

    @pl.when(convolver)
    def _():
        def greet(i, carry):
            pl.semaphore_signal(barrier, inc=1, device_id={"ka": lax.rem(me + i, n_ka)}, device_id_type=MESH)
            return carry

        lax.fori_loop(1, n_ka, greet, 0)

    for d in range(1, n_hist):
        pl.semaphore_signal(barrier, inc=1, device_id={"hist": lax.rem(hist + d, n_hist)}, device_id_type=MESH)

    step_copy = pltpu.make_async_copy(step_hbm, step_ref, table_sem.at[0])
    table_copy = pltpu.make_async_copy(table_hbm, table_v, table_sem.at[1])
    chunks = 4
    width = 16 // chunks
    sh_copies = [
        pltpu.make_async_copy(
            sh_hbm.at[:, :, pl.ds(q * width, width)], sh_v.at[:, :, pl.ds(q * width, width)], sh_sem.at[q]
        )
        for q in range(chunks)
    ]
    gh_copies = [
        pltpu.make_async_copy(
            gh_hbm.at[:, :, pl.ds(q * width, width)], gh_v.at[:, :, pl.ds(q * width, width)], gh_sem.at[q]
        )
        for q in range(chunks)
    ]
    for copy in [step_copy] + sh_copies + [table_copy] + gh_copies:
        copy.start()

    for a in range(2):
        for part in range(2):
            r = 2 * a + part
            row_copies[r].wait()
            for ph in range(2):
                turned[2 * r + ph] = rows_v[a, part, pl.ds(128 * ph, 128), :].T
    for r in range(4):
        for ph in range(2):
            send_rows[pl.ds(4 * ph + r, slab, stride=8), :] = turned[2 * r + ph, pl.ds(slab * hist, slab), :]

    def tile(i):
        return pl.ds(pl.multiple_of(8 * i, 8), 8)

    def send_row(to):
        pltpu.make_async_remote_copy(
            src_ref=send_rows.at[tile(to)], dst_ref=recv_rows.at[tile(me)], send_sem=send_sem.at[0],
            recv_sem=recv_sem.at[0], device_id={"ka": to}, device_id_type=MESH,
        ).start()

    some_rows = recv_rows.at[pl.ds(0, 8 * (n_conv - 1))]
    all_rows = recv_rows.at[pl.ds(0, 8 * n_conv)]
    other_rows = recv_rows.at[pl.ds(0, 8 * (n_ka - 1))]
    some_sig = recv_sig.at[:, pl.ds(0, n_conv - 1)]

    @pl.when(convolver)
    def _():
        own = pltpu.make_async_copy(send_rows.at[tile(me)], recv_rows.at[tile(me)], self_sem.at[0])
        own.start()
        pl.semaphore_wait(barrier, n_conv - 1 + n_hist - 1)

        def go(i, carry):
            send_row(lax.rem(me + i, n_conv))
            return carry

        lax.fori_loop(1, n_conv, go, 0)
        own.wait()

    @pl.when(jnp.logical_not(convolver))
    def _():
        pl.semaphore_wait(barrier, n_conv + n_hist - 1)

        def go(i, carry):
            send_row(lax.rem(me + i, n_conv))
            return carry

        lax.fori_loop(0, n_conv, go, 0)

    step_copy.wait()
    lane = lax.broadcasted_iota(jnp.int32, (1, 128), 1)
    place = lane // 32
    alive = (hist * slab + lane % 32) < step_ref[0]

    def spread(left, pieces):
        for part in range(2):
            for a in range(NORB):
                row = pieces(part, a, 0)
                for b in range(1, NORB):
                    row = jnp.where(place == b, pieces(part, a, b), row)
                row = jnp.where(alive, row, 0.0)
                left[part, pl.ds(a, 16, stride=8), :] = -row if part else row
                left[1 - part, pl.ds(4 + a, 16, stride=8), :] = row

    def green_piece(part, a, b):
        block = rows_v[0, part, pl.ds((4 * a + b) * 16, 16), :]
        return pltpu.roll(block, lax.rem(32 * b + 128 - 32 * hist, 128), 1)

    def left_of(left, k):
        at = pl.ds(8 * k, 8)
        return jnp.concatenate([left[0, at, :], left[1, at, :]], axis=1).astype(BF16)

    spread(left_g, green_piece)

    s_at = lax.broadcasted_iota(jnp.int32, (slab, 128), 0) + hist * slab
    t_at = lax.broadcasted_iota(jnp.int32, (slab, 128), 1)
    lower = jnp.where(s_at >= t_at, 1.0, 0.0).astype(BF16)

    def history(ref, k):
        return jnp.concatenate(
            [
                jnp.concatenate(
                    [ref[part, 4 * b + c, k] * lower for part in range(2) for b in range(NORB)], axis=0
                )
                for c in range(NORB)
            ],
            axis=1,
        )

    for q in range(chunks):
        sh_copies[q].wait()
        for kk in range(width):
            k = q * width + kk
            partial[k] = dot(left_of(left_g, k), history(sh_v, k))

    table_copy.wait()

    @pl.when(convolver)
    def _():
        pltpu.make_async_copy(other_rows, other_rows, recv_sem.at[0]).wait()

        def block(ph, a, part, half):
            return recv_rows[pl.ds(8 * half + 4 * ph + 2 * a + part, 32, stride=16), :]

        sigma = convolve(block, table_v).astype(BF16)
        for ph in range(2):
            for half in range(2):
                at = 128 * (2 * ph + half)
                send_sig[half, ph] = sigma[:, at : at + 128].reshape(LX, 2, 128)

        def send_sigma(i, carry):
            to = 8 * (i // 8) + lax.rem(me + i, 8)

            @pl.when(to != me)
            def _():
                pltpu.make_async_remote_copy(
                    src_ref=send_sig.at[lax.rem(to, 2), :, to // 2], dst_ref=recv_sig.at[:, me],
                    send_sem=send_sem.at[1], recv_sem=recv_sem.at[1], device_id={"ka": to}, device_id_type=MESH,
                ).start()

            return carry

        lax.fori_loop(0, n_ka, send_sigma, 0)
        own = pltpu.make_async_copy(send_sig.at[lax.rem(me, 2), :, me // 2], recv_sig.at[:, me], self_sem.at[1])
        own.start()
        own.wait()
        pltpu.make_async_copy(some_sig, some_sig, recv_sem.at[1]).wait()

    @pl.when(jnp.logical_not(convolver))
    def _():
        pltpu.make_async_copy(recv_sig, recv_sig, recv_sem.at[1]).wait()

    wide_sig[...] = recv_sig[...].reshape(2, 2 * LX, 128).astype(F32)
    stacked = jnp.concatenate(
        [wide_sig[ph, pl.ds(part, 32, stride=2), :] for part in range(2) for ph in range(2)], axis=0
    ).T

    def sigma_piece(part, a, b):
        ph = a // 2
        at = ((a % 2) * 4 + b) * 16
        shift = (32 * (b - 2 * part - ph)) % 128
        rows = stacked[at : at + 16]
        return pltpu.roll(rows, shift, 1) if shift else rows

    spread(left_s, sigma_piece)

    for q in range(chunks):
        gh_copies[q].wait()
        rows = [[] for _ in range(NORB)]
        for kk in range(width):
            k = q * width + kk
            total = partial[k] + dot(left_of(left_s, k), history(gh_v, k))
            columns = [total[:, 128 * c : 128 * c + 128] for c in range(NORB)]
            for to in range(NORB):
                row = None
                for c in range(NORB):
                    shift = (32 * (c - to)) % 128
                    moved = pltpu.roll(columns[c], shift, 1) if shift else columns[c]
                    row = moved if row is None else jnp.where(place == c, moved, row)
                rows[to].append(row)
        for to in range(NORB):
            full = jnp.concatenate(rows[to], axis=0)
            rs_full[to, q] = full
            rs_send[to, q] = full.astype(BF16)
        for d in (2, 1, 3):
            to = lax.rem(hist + d, n_hist)
            pltpu.make_async_remote_copy(
                src_ref=rs_send.at[to, q], dst_ref=rs_recv.at[n_hist - 1 - d, q],
                send_sem=send_sem.at[2], recv_sem=recv_sem.at[2], device_id={"hist": to}, device_id_type=MESH,
            ).start()

    pltpu.make_async_copy(rs_recv, rs_recv, recv_sem.at[2]).wait()
    scale = 2.0 / (n_hist * slab)
    got = [rs_recv[i].reshape(128, 128).astype(F32) for i in range(3)]
    summed[...] = ((got[0] + got[1]) + (got[2] + rs_full[hist].reshape(128, 128))) * scale
    for m in range(8):
        rows = summed[pl.ds(m, 16, stride=8), :]
        for c in range(NORB):
            moved = pltpu.roll(rows, 128 - 32 * c, 1) if c else rows
            out_ref[m // 4, (m % 4) * 4 + c] = moved[:, :slab]

    pltpu.make_async_copy(rs_recv, rs_recv, send_sem.at[2]).wait()

    @pl.when(convolver)
    def _():
        pltpu.make_async_copy(some_rows, some_rows, send_sem.at[0]).wait()
        pltpu.make_async_copy(recv_sig, recv_sig, send_sem.at[1]).wait()
        pltpu.make_async_copy(some_sig, some_sig, send_sem.at[1]).wait()

    @pl.when(jnp.logical_not(convolver))
    def _():
        pltpu.make_async_copy(all_rows, all_rows, send_sem.at[0]).wait()


def per_device(n_ka, n_hist, g_row, w_row, g_hist, s_hist, step_now):
    rows = [jnp.transpose(x, (0, 1, 3, 2)).reshape(2, PAIRS * 16, 128) for x in (g_row, w_row)]
    table = jnp.asarray(tables())
    return pl.pallas_call(
        functools.partial(kernel, n_ka, n_hist),
        out_shape=jax.ShapeDtypeStruct((2, PAIRS, 16, 32), F32),
        in_specs=[pl.BlockSpec(memory_space=pl.ANY)] * 6,
        out_specs=pl.BlockSpec(memory_space=pltpu.VMEM),
        scratch_shapes=[
            pltpu.SMEM((1,), jnp.int32),
            pltpu.VMEM((2, 2, 256, 128), F32),
            pltpu.VMEM((2, 16, 16, 32, 128), BF16),
            pltpu.VMEM((2, 16, 16, 32, 128), BF16),
            pltpu.VMEM(table.shape, BF16),
            pltpu.VMEM((8, 128, 128), F32),
            pltpu.VMEM((256, 128), F32),
            pltpu.VMEM((512, 128), F32),
            pltpu.VMEM((2, 2, 32, 2, 128), BF16),
            pltpu.VMEM((2, 32, 2, 128), BF16),
            pltpu.VMEM((2, 64, 128), F32),
            pltpu.VMEM((2, 128, 128), F32),
            pltpu.VMEM((2, 128, 128), F32),
            pltpu.VMEM((16, 8, 512), F32),
            pltpu.VMEM((4, 4, 32, 128), F32),
            pltpu.VMEM((4, 4, 32, 128), BF16),
            pltpu.VMEM((3, 4, 32, 128), BF16),
            pltpu.VMEM((128, 128), F32),
            pltpu.SemaphoreType.DMA((2, 2)),
            pltpu.SemaphoreType.DMA((2,)),
            pltpu.SemaphoreType.DMA((4,)),
            pltpu.SemaphoreType.DMA((4,)),
            pltpu.SemaphoreType.DMA((2,)),
            pltpu.SemaphoreType.DMA((3,)),
            pltpu.SemaphoreType.DMA((3,)),
        ],
        compiler_params=pltpu.CompilerParams(
            collective_id=0, has_side_effects=True, vmem_limit_bytes=LIMIT * 1024
        ),
    )(step_now, *rows, g_hist, s_hist, table)


def solution(mesh):
    placed = (
        P(None, None, None, "ka"),
        P(None, None, None, "ka"),
        P(None, None, "ka", "hist", None),
        P(None, None, "ka", "hist", None),
        P(),
    )
    return jax.shard_map(
        functools.partial(per_device, mesh.shape["ka"], mesh.shape["hist"]),
        mesh=mesh,
        in_specs=placed,
        out_specs=P(None, None, "ka", "hist"),
        check_vma=False,
    )
```

time: 36.2 us -> 32.5 us (0.90)
  Pallas kernels: 33.7 us -> 31.1 us
  local copies, waits for them, and re-layouts: 1.67 us -> 0.71 us
    pallas_call x1, Pallas kernels: 33.7 us -> 31.1 us  [per_device(): pl.pallas_call(functools.partial(kernel, n_ka, n_hist), out_shape=jax.Sha...]
    unnamed x1, local copies, waits for them, and re-layouts: 1.67 us -> 0.71 us
where the time goes in v1:
time: 32.5 us
  Pallas kernels  31.1 us (96%)
  local copies, waits for them, and re-layouts  0.71 us (2%)
  between operations  0.66 us (2%)
    pallas_call x1, Pallas kernels, per_device(): pl.pallas_call(functools.partial(kernel, n_ka, n_hist), out_shape=jax.Sha...  31.1 us
    unnamed x1, local copies, waits for them, and re-layouts  0.71 us

profile of v1, /device:TPU:1, one launch (start us, length us, event | category | flops | bytes accessed | tf_op | source)
XLA Modules:
  0.0 32.5 jit_solution(15639756545796481845)
XLA Ops:
  0.7 31.1 %shard_map.64 = f32[2,16,16,32]{3,2,1,0:T(8,128)S(1)} custom-call(s32[1]{0:T(128)S(6)} %copy.8.step_hbm, f32[2,256,128]{2,1,0:T(8,128)} %bitcast.6, f32[2,256,128]{2,1,0:T(8,128)} %bitcast.7, bf16[2,16,16,32,128]{4,3,2,1,0:T(8,128)(2,1)} %gh_hbm.1, bf16[2,16,16,32,128]{4,3,2,1,0:T(8,128)(2,1)} %sh_hbm.1, bf16[1152,512]{1,0:T(8,128)(2,1)} %constant.2.clone.table_hbm), custom_call_target="tpu_custom_call" | custom-call | tf_op jit(solution)/shard_map/pallas_call | solution.py:353
  31.8 0.7 %copy.9 = f32[2,16,16,32]{3,2,1,0:T(8,128)} copy(f32[2,16,16,32]{3,2,1,0:T(8,128)S(1)} %shard_map.64) | data formatting | bytes 131072

commit v2 on v1

--- a/solution.py
+++ b/solution.py
@@ -107,7 +107,7 @@
     step_hbm, g_hbm, w_hbm, gh_hbm, sh_hbm, table_hbm,
     out_ref,
     step_ref, rows_v, gh_v, sh_v, table_v,
-    turned, send_rows, recv_rows, send_sig, recv_sig, wide_sig, left_g, left_s, partial, rs_full, rs_send, rs_recv, summed,
+    turned, send_rows, send_half, recv_rows, recv_half, send_sig, recv_sig, wide_sig, left_g, left_s, partial, rs_full, rs_send, rs_recv, summed,
     row_sem, table_sem, sh_sem, gh_sem, self_sem, send_sem, recv_sem,
 ):
     hist = lax.axis_index("hist")
@@ -168,15 +168,13 @@
     def tile(i):
         return pl.ds(pl.multiple_of(8 * i, 8), 8)
 
-    def send_row(to):
+    def send_row(to, src, dst, at, which):
         pltpu.make_async_remote_copy(
-            src_ref=send_rows.at[tile(to)], dst_ref=recv_rows.at[tile(me)], send_sem=send_sem.at[0],
-            recv_sem=recv_sem.at[0], device_id={"ka": to}, device_id_type=MESH,
+            src_ref=src.at[tile(to)], dst_ref=dst.at[tile(at)], send_sem=send_sem.at[which],
+            recv_sem=recv_sem.at[which], device_id={"ka": to}, device_id_type=MESH,
         ).start()
 
     some_rows = recv_rows.at[pl.ds(0, 8 * (n_conv - 1))]
-    all_rows = recv_rows.at[pl.ds(0, 8 * n_conv)]
-    other_rows = recv_rows.at[pl.ds(0, 8 * (n_ka - 1))]
     some_sig = recv_sig.at[:, pl.ds(0, n_conv - 1)]
 
     @pl.when(convolver)
@@ -186,7 +184,7 @@
         pl.semaphore_wait(barrier, n_conv - 1 + n_hist - 1)
 
         def go(i, carry):
-            send_row(lax.rem(me + i, n_conv))
+            send_row(lax.rem(me + i, n_conv), send_rows, recv_rows, me, 0)
             return carry
 
         lax.fori_loop(1, n_conv, go, 0)
@@ -194,10 +192,11 @@
 
     @pl.when(jnp.logical_not(convolver))
     def _():
+        send_half[...] = send_rows[...].astype(BF16)
         pl.semaphore_wait(barrier, n_conv + n_hist - 1)
 
         def go(i, carry):
-            send_row(lax.rem(me + i, n_conv))
+            send_row(lax.rem(me + i, n_conv), send_half, recv_half, me - n_conv, 3)
             return carry
 
         lax.fori_loop(0, n_conv, go, 0)
@@ -252,7 +251,9 @@
 
     @pl.when(convolver)
     def _():
-        pltpu.make_async_copy(other_rows, other_rows, recv_sem.at[0]).wait()
+        pltpu.make_async_copy(some_rows, some_rows, recv_sem.at[0]).wait()
+        pltpu.make_async_copy(recv_half, recv_half, recv_sem.at[3]).wait()
+        recv_rows[pl.ds(8 * n_conv, 8 * n_conv), :] = recv_half[...].astype(F32)
 
         def block(ph, a, part, half):
             return recv_rows[pl.ds(8 * half + 4 * ph + 2 * a + part, 32, stride=16), :]
@@ -344,7 +345,7 @@
 
     @pl.when(jnp.logical_not(convolver))
     def _():
-        pltpu.make_async_copy(all_rows, all_rows, send_sem.at[0]).wait()
+        pltpu.make_async_copy(recv_half, recv_half, send_sem.at[3]).wait()
 
 
 def per_device(n_ka, n_hist, g_row, w_row, g_hist, s_hist, step_now):
@@ -363,7 +364,9 @@
             pltpu.VMEM(table.shape, BF16),
             pltpu.VMEM((8, 128, 128), F32),
             pltpu.VMEM((256, 128), F32),
+            pltpu.VMEM((256, 128), BF16),
             pltpu.VMEM((512, 128), F32),
+            pltpu.VMEM((256, 128), BF16),
             pltpu.VMEM((2, 2, 32, 2, 128), BF16),
             pltpu.VMEM((2, 32, 2, 128), BF16),
             pltpu.VMEM((2, 64, 128), F32),
@@ -379,8 +382,8 @@
             pltpu.SemaphoreType.DMA((4,)),
             pltpu.SemaphoreType.DMA((4,)),
             pltpu.SemaphoreType.DMA((2,)),
-            pltpu.SemaphoreType.DMA((3,)),
-            pltpu.SemaphoreType.DMA((3,)),
+            pltpu.SemaphoreType.DMA((4,)),
+            pltpu.SemaphoreType.DMA((4,)),
         ],
         compiler_params=pltpu.CompilerParams(
             collective_id=0, has_side_effects=True, vmem_limit_bytes=LIMIT * 1024

time: 32.5 us -> 29.9 us (0.920)
  Pallas kernels: 31.1 us -> 28.5 us
    pallas_call x1, Pallas kernels: 31.1 us -> 28.5 us  [per_device(): pl.pallas_call(functools.partial(kernel, n_ka, n_hist), out_shape=jax.Sha...]
where the time goes in v2:
time: 29.9 us; the launch traced here: 29.8 us
  Pallas kernels  28.5 us (95%)
  local copies, waits for them, and re-layouts  0.71 us (2%)
  between operations  0.66 us (2%)
    pallas_call x1, Pallas kernels, per_device(): pl.pallas_call(functools.partial(kernel, n_ka, n_hist), out_shape=jax.Sha...  28.5 us
    unnamed x1, local copies, waits for them, and re-layouts  0.71 us

profile of v2, /device:TPU:1, one launch (start us, length us, event | category | flops | bytes accessed | tf_op | source)
XLA Modules:
  0.0 29.8 jit_solution(3242162057870718071)
XLA Ops:
  0.7 28.5 %shard_map.64 = f32[2,16,16,32]{3,2,1,0:T(8,128)S(1)} custom-call(s32[1]{0:T(128)S(6)} %copy.8.step_hbm, f32[2,256,128]{2,1,0:T(8,128)} %bitcast.6, f32[2,256,128]{2,1,0:T(8,128)} %bitcast.7, bf16[2,16,16,32,128]{4,3,2,1,0:T(8,128)(2,1)} %gh_hbm.1, bf16[2,16,16,32,128]{4,3,2,1,0:T(8,128)(2,1)} %sh_hbm.1, bf16[1152,512]{1,0:T(8,128)(2,1)} %constant.2.clone.table_hbm), custom_call_target="tpu_custom_call" | custom-call | tf_op jit(solution)/shard_map/pallas_call | solution.py:354
  29.1 0.7 %copy.9 = f32[2,16,16,32]{3,2,1,0:T(8,128)} copy(f32[2,16,16,32]{3,2,1,0:T(8,128)S(1)} %shard_map.64) | data formatting | bytes 131072

commit v3 on v2

--- a/solution.py
+++ b/solution.py
@@ -29,9 +29,11 @@
     step = np.arange(LX)
     theta = 2.0 * math.pi * (step[:, None] * step[None, :] % LX) / LX
     cosine, sine = np.cos(theta), np.sin(theta)
-    first = np.block([[cosine, sine], [-sine, cosine]])
-    high, low = split_table(first)
-    first = np.concatenate([high, low, high], axis=1)
+    first = np.block([[cosine, sine], [-sine, cosine]]).reshape(2 * LX, 2, 2, LX // 2)
+    firsts = []
+    for half in range(2):
+        high, low = split_table(first[:, :, half].reshape(2 * LX, LX))
+        firsts.append(np.concatenate([high, low, high], axis=1))
     last = np.stack(
         [np.concatenate([-sine, -cosine], 1), np.concatenate([cosine, -sine], 1)],
         axis=1,
@@ -47,7 +49,7 @@
     forth = np.concatenate([along(cosine), along(sine)], axis=1)
     back = np.concatenate([along(cosine).T, along(sine).T], axis=1)
     ends = np.zeros((128, 512), ml_dtypes.bfloat16)
-    ends[:64, :192], ends[64:, :192] = first, last
+    ends[:64, :96], ends[:64, 128:224], ends[64:, :192] = firsts[0], firsts[1], last
     return np.concatenate(split_table(forth) + split_table(back) + (ends,), axis=0)
 
 
@@ -68,30 +70,40 @@
     return both[:rows] + both[rows:] + dot(high, right_low)
 
 
-def convolve(block, table):
-    first, last = table[1024:1088, :192], table[1088:1152, :192]
-    forth = table[0:256, :], table[256:512, :]
+def along_ky(stage):
+    columns = []
+    for i in range(4):
+        re, im = stage[32 * i : 32 * i + 16], stage[32 * i + 16 : 32 * i + 32]
+        columns.append(jnp.concatenate([re[:, :256] + im[:, 256:], im[:, :256] - re[:, 256:]], axis=0))
+    high, low = cut(jnp.concatenate(columns, axis=1))
+    return jnp.concatenate([high, high, low], axis=0)
+
+
+def gather(rows, start):
+    return jnp.concatenate(
+        [
+            jnp.concatenate([rows[pl.ds(start + 8 * half + r, 16, stride=16), :] for half in range(2)], axis=1)
+            for r in range(8)
+        ],
+        axis=0,
+    )
+
+
+def early_part(rows, table):
+    stage = fine_dot(gather(rows, 0), table[0:256, :], table[256:512, :])
+    return dot(table[1024:1088, 0:96], along_ky(stage))
+
+
+def convolve(early, rows, table):
+    late = gather(rows, 256).astype(BF16)
+    stage = dot(late, table[0:256, :]) + dot(late, table[256:512, :])
+    stage = early + dot(table[1024:1088, 128:224], along_ky(stage))
     back = table[512:768, :], table[768:1024, :]
-    data = jnp.concatenate(
-        [
-            jnp.concatenate([block(ph, a, 0, half), block(ph, a, 1, half)], axis=0)
-            for ph in range(2)
-            for a in range(2)
-            for half in range(2)
-        ],
-        axis=1,
-    )
-    high, low = cut(data)
-    stage = dot(first, jnp.concatenate([high, high, low], axis=0))
-    stage = jnp.concatenate([stage[:, 256 * i : 256 * i + 256] for i in range(4)], axis=0)
-    stage = fine_dot(stage, *forth)
+    last = table[1088:1152, :192]
     prods = []
     for ph in range(2):
-        parts = []
-        for i in (2 * ph, 2 * ph + 1):
-            re, im = stage[64 * i : 64 * i + 32], stage[64 * i + 32 : 64 * i + 64]
-            parts.append((re[:, :256] + im[:, 256:], im[:, :256] - re[:, 256:]))
-        (g_re, g_im), (w_re, w_im) = parts
+        g, w = stage[:, 512 * ph : 512 * ph + 256], stage[:, 512 * ph + 256 : 512 * ph + 512]
+        (g_re, g_im), (w_re, w_im) = (g[:32], g[32:]), (w[:32], w[32:])
         prods += [g_re * w_re - g_im * w_im, g_re * w_im + g_im * w_re]
     stage = fine_dot(jnp.concatenate(prods, axis=0), *back)
     wide = []
@@ -108,7 +120,7 @@
     out_ref,
     step_ref, rows_v, gh_v, sh_v, table_v,
     turned, send_rows, send_half, recv_rows, recv_half, send_sig, recv_sig, wide_sig, left_g, left_s, partial, rs_full, rs_send, rs_recv, summed,
-    row_sem, table_sem, sh_sem, gh_sem, self_sem, send_sem, recv_sem,
+    row_sem, table_sem, sh_sem, gh_sem, self_sem, send_sem, recv_sem, plane_sem, all_sem,
 ):
     hist = lax.axis_index("hist")
     me = lax.axis_index("ka")
@@ -128,13 +140,14 @@
     @pl.when(convolver)
     def _():
         def greet(i, carry):
-            pl.semaphore_signal(barrier, inc=1, device_id={"ka": lax.rem(me + i, n_ka)}, device_id_type=MESH)
+            to = lax.rem(me + i, n_ka)
+            pl.semaphore_signal(barrier, inc=1, device_id={"ka": to}, device_id_type=MESH)
             return carry
 
         lax.fori_loop(1, n_ka, greet, 0)
 
-    for d in range(1, n_hist):
-        pl.semaphore_signal(barrier, inc=1, device_id={"hist": lax.rem(hist + d, n_hist)}, device_id_type=MESH)
+        for d in range(1, n_hist):
+            pl.semaphore_signal(barrier, inc=1, device_id={"hist": lax.rem(hist + d, n_hist)}, device_id_type=MESH)
 
     step_copy = pltpu.make_async_copy(step_hbm, step_ref, table_sem.at[0])
     table_copy = pltpu.make_async_copy(table_hbm, table_v, table_sem.at[1])
@@ -193,10 +206,10 @@
     @pl.when(jnp.logical_not(convolver))
     def _():
         send_half[...] = send_rows[...].astype(BF16)
-        pl.semaphore_wait(barrier, n_conv + n_hist - 1)
+        pl.semaphore_wait(barrier, n_conv)
 
         def go(i, carry):
-            send_row(lax.rem(me + i, n_conv), send_half, recv_half, me - n_conv, 3)
+            send_row(lax.rem(me + n_conv - i, n_conv), send_half, recv_half, me - n_conv, 3)
             return carry
 
         lax.fori_loop(0, n_conv, go, 0)
@@ -230,11 +243,11 @@
     t_at = lax.broadcasted_iota(jnp.int32, (slab, 128), 1)
     lower = jnp.where(s_at >= t_at, 1.0, 0.0).astype(BF16)
 
-    def history(ref, k):
+    def history(ref, k, factor):
         return jnp.concatenate(
             [
                 jnp.concatenate(
-                    [ref[part, 4 * b + c, k] * lower for part in range(2) for b in range(NORB)], axis=0
+                    [factor(ref[part, 4 * b + c, k]) for part in range(2) for b in range(NORB)], axis=0
                 )
                 for c in range(NORB)
             ],
@@ -245,20 +258,31 @@
         sh_copies[q].wait()
         for kk in range(width):
             k = q * width + kk
-            partial[k] = dot(left_of(left_g, k), history(sh_v, k))
+            partial[k] = dot(left_of(left_g, k), history(sh_v, k, lambda x: x * lower))
+
+    for q in range(chunks):
+        gh_copies[q].wait()
+
+        def mask(i, carry):
+            part, p = i // PAIRS, lax.rem(i, PAIRS)
+            for kk in range(width):
+                k = q * width + kk
+                gh_v[part, p, k] = gh_v[part, p, k] * lower
+            return carry
+
+        lax.fori_loop(0, 2 * PAIRS, mask, 0)
 
     table_copy.wait()
 
     @pl.when(convolver)
     def _():
         pltpu.make_async_copy(some_rows, some_rows, recv_sem.at[0]).wait()
+        early = early_part(recv_rows, table_v)
         pltpu.make_async_copy(recv_half, recv_half, recv_sem.at[3]).wait()
+        for d in range(1, n_hist):
+            pl.semaphore_signal(plane_sem, inc=1, device_id={"hist": lax.rem(hist + d, n_hist)}, device_id_type=MESH)
         recv_rows[pl.ds(8 * n_conv, 8 * n_conv), :] = recv_half[...].astype(F32)
-
-        def block(ph, a, part, half):
-            return recv_rows[pl.ds(8 * half + 4 * ph + 2 * a + part, 32, stride=16), :]
-
-        sigma = convolve(block, table_v).astype(BF16)
+        sigma = convolve(early, recv_rows, table_v).astype(BF16)
         for ph in range(2):
             for half in range(2):
                 at = 128 * (2 * ph + half)
@@ -279,12 +303,15 @@
         lax.fori_loop(0, n_ka, send_sigma, 0)
         own = pltpu.make_async_copy(send_sig.at[lax.rem(me, 2), :, me // 2], recv_sig.at[:, me], self_sem.at[1])
         own.start()
+        pl.semaphore_wait(plane_sem, n_hist - 1)
+        pl.semaphore_signal(all_sem, inc=1, device_id={"ka": me + n_conv}, device_id_type=MESH)
         own.wait()
         pltpu.make_async_copy(some_sig, some_sig, recv_sem.at[1]).wait()
 
     @pl.when(jnp.logical_not(convolver))
     def _():
         pltpu.make_async_copy(recv_sig, recv_sig, recv_sem.at[1]).wait()
+        pl.semaphore_wait(all_sem, 1)
 
     wide_sig[...] = recv_sig[...].reshape(2, 2 * LX, 128).astype(F32)
     stacked = jnp.concatenate(
@@ -301,11 +328,10 @@
     spread(left_s, sigma_piece)
 
     for q in range(chunks):
-        gh_copies[q].wait()
         rows = [[] for _ in range(NORB)]
         for kk in range(width):
             k = q * width + kk
-            total = partial[k] + dot(left_of(left_s, k), history(gh_v, k))
+            total = partial[k] + dot(left_of(left_s, k), history(gh_v, k, lambda x: x))
             columns = [total[:, 128 * c : 128 * c + 128] for c in range(NORB)]
             for to in range(NORB):
                 row = None
@@ -384,6 +410,8 @@
             pltpu.SemaphoreType.DMA((2,)),
             pltpu.SemaphoreType.DMA((4,)),
             pltpu.SemaphoreType.DMA((4,)),
+            pltpu.SemaphoreType.REGULAR,
+            pltpu.SemaphoreType.REGULAR,
         ],
         compiler_params=pltpu.CompilerParams(
             collective_id=0, has_side_effects=True, vmem_limit_bytes=LIMIT * 1024

time: 29.9 us -> 29 us (0.970)
  Pallas kernels: 28.5 us -> 27.6 us
    pallas_call x1, Pallas kernels: 28.5 us -> 27.6 us  [per_device(): pl.pallas_call(functools.partial(kernel, n_ka, n_hist), out_shape=jax.Sha...]
where the time goes in v3:
time: 29 us
  Pallas kernels  27.6 us (95%)
  local copies, waits for them, and re-layouts  0.71 us (2%)
  between operations  0.66 us (2%)
    pallas_call x1, Pallas kernels, per_device(): pl.pallas_call(functools.partial(kernel, n_ka, n_hist), out_shape=jax.Sha...  27.6 us
    unnamed x1, local copies, waits for them, and re-layouts  0.71 us

profile of v3, /device:TPU:1, one launch (start us, length us, event | category | flops | bytes accessed | tf_op | source)
XLA Modules:
  0.0 29.0 jit_solution(16799829783740183232)
XLA Ops:
  0.7 27.6 %shard_map.64 = f32[2,16,16,32]{3,2,1,0:T(8,128)S(1)} custom-call(s32[1]{0:T(128)S(6)} %copy.8.step_hbm, f32[2,256,128]{2,1,0:T(8,128)} %bitcast.6, f32[2,256,128]{2,1,0:T(8,128)} %bitcast.7, bf16[2,16,16,32,128]{4,3,2,1,0:T(8,128)(2,1)} %gh_hbm.1, bf16[2,16,16,32,128]{4,3,2,1,0:T(8,128)(2,1)} %sh_hbm.1, bf16[1152,512]{1,0:T(8,128)(2,1)} %constant.2.clone.table_hbm), custom_call_target="tpu_custom_call" | custom-call | tf_op jit(solution)/shard_map/pallas_call | solution.py:380
  28.3 0.7 %copy.9 = f32[2,16,16,32]{3,2,1,0:T(8,128)} copy(f32[2,16,16,32]{3,2,1,0:T(8,128)S(1)} %shard_map.64) | data formatting | bytes 131072

commit v4 on v3

--- a/solution.py
+++ b/solution.py
@@ -151,7 +151,7 @@
 
     step_copy = pltpu.make_async_copy(step_hbm, step_ref, table_sem.at[0])
     table_copy = pltpu.make_async_copy(table_hbm, table_v, table_sem.at[1])
-    chunks = 4
+    chunks = 1
     width = 16 // chunks
     sh_copies = [
         pltpu.make_async_copy(
@@ -399,14 +399,14 @@
             pltpu.VMEM((2, 128, 128), F32),
             pltpu.VMEM((2, 128, 128), F32),
             pltpu.VMEM((16, 8, 512), F32),
-            pltpu.VMEM((4, 4, 32, 128), F32),
-            pltpu.VMEM((4, 4, 32, 128), BF16),
-            pltpu.VMEM((3, 4, 32, 128), BF16),
+            pltpu.VMEM((4, 1, 128, 128), F32),
+            pltpu.VMEM((4, 1, 128, 128), BF16),
+            pltpu.VMEM((3, 1, 128, 128), BF16),
             pltpu.VMEM((128, 128), F32),
             pltpu.SemaphoreType.DMA((2, 2)),
             pltpu.SemaphoreType.DMA((2,)),
-            pltpu.SemaphoreType.DMA((4,)),
-            pltpu.SemaphoreType.DMA((4,)),
+            pltpu.SemaphoreType.DMA((1,)),
+            pltpu.SemaphoreType.DMA((1,)),
             pltpu.SemaphoreType.DMA((2,)),
             pltpu.SemaphoreType.DMA((4,)),
             pltpu.SemaphoreType.DMA((4,)),

time: 29 us -> 28.5 us (0.983)
  Pallas kernels: 27.6 us -> 27.1 us
    pallas_call x1, Pallas kernels: 27.6 us -> 27.1 us  [per_device(): pl.pallas_call(functools.partial(kernel, n_ka, n_hist), out_shape=jax.Sha...]
where the time goes in v4:
time: 28.5 us
  Pallas kernels  27.1 us (95%)
  local copies, waits for them, and re-layouts  0.71 us (2%)
  between operations  0.66 us (2%)
    pallas_call x1, Pallas kernels, per_device(): pl.pallas_call(functools.partial(kernel, n_ka, n_hist), out_shape=jax.Sha...  27.1 us
    unnamed x1, local copies, waits for them, and re-layouts  0.71 us

profile of v4, /device:TPU:1, one launch (start us, length us, event | category | flops | bytes accessed | tf_op | source)
XLA Modules:
  0.0 28.5 jit_solution(11997415206729569119)
XLA Ops:
  0.7 27.1 %shard_map.64 = f32[2,16,16,32]{3,2,1,0:T(8,128)S(1)} custom-call(s32[1]{0:T(128)S(6)} %copy.8.step_hbm, f32[2,256,128]{2,1,0:T(8,128)} %bitcast.6, f32[2,256,128]{2,1,0:T(8,128)} %bitcast.7, bf16[2,16,16,32,128]{4,3,2,1,0:T(8,128)(2,1)} %gh_hbm.1, bf16[2,16,16,32,128]{4,3,2,1,0:T(8,128)(2,1)} %sh_hbm.1, bf16[1152,512]{1,0:T(8,128)(2,1)} %constant.2.clone.table_hbm), custom_call_target="tpu_custom_call" | custom-call | tf_op jit(solution)/shard_map/pallas_call | solution.py:380
  27.7 0.7 %copy.9 = f32[2,16,16,32]{3,2,1,0:T(8,128)} copy(f32[2,16,16,32]{3,2,1,0:T(8,128)S(1)} %shard_map.64) | data formatting | bytes 131072

commit v5 on v4

--- a/solution.py
+++ b/solution.py
@@ -209,7 +209,7 @@
         pl.semaphore_wait(barrier, n_conv)
 
         def go(i, carry):
-            send_row(lax.rem(me + n_conv - i, n_conv), send_half, recv_half, me - n_conv, 3)
+            send_row(8 * lax.rem(me // 8 + 8 - i // 8, 4) + lax.rem(me + i, 8), send_half, recv_half, me - n_conv, 3)
             return carry
 
         lax.fori_loop(0, n_conv, go, 0)

time: 28.5 us -> 28.5 us (level)
  no operation moved by 1% of the time
where the time goes in v5:
time: 28.5 us; the launch traced here: 28.4 us
  Pallas kernels  27.1 us (95%)
  local copies, waits for them, and re-layouts  0.71 us (2%)
  between operations  0.66 us (2%)
    pallas_call x1, Pallas kernels, per_device(): pl.pallas_call(functools.partial(kernel, n_ka, n_hist), out_shape=jax.Sha...  27.1 us
    unnamed x1, local copies, waits for them, and re-layouts  0.71 us

profile of v5, /device:TPU:1, one launch (start us, length us, event | category | flops | bytes accessed | tf_op | source)
XLA Modules:
  0.0 28.4 jit_solution(4764220102753279072)
XLA Ops:
  0.7 27.1 %shard_map.64 = f32[2,16,16,32]{3,2,1,0:T(8,128)S(1)} custom-call(s32[1]{0:T(128)S(6)} %copy.8.step_hbm, f32[2,256,128]{2,1,0:T(8,128)} %bitcast.6, f32[2,256,128]{2,1,0:T(8,128)} %bitcast.7, bf16[2,16,16,32,128]{4,3,2,1,0:T(8,128)(2,1)} %gh_hbm.1, bf16[2,16,16,32,128]{4,3,2,1,0:T(8,128)(2,1)} %sh_hbm.1, bf16[1152,512]{1,0:T(8,128)(2,1)} %constant.2.clone.table_hbm), custom_call_target="tpu_custom_call" | custom-call | tf_op jit(solution)/shard_map/pallas_call | solution.py:380
  27.7 0.7 %copy.9 = f32[2,16,16,32]{3,2,1,0:T(8,128)} copy(f32[2,16,16,32]{3,2,1,0:T(8,128)S(1)} %shard_map.64) | data formatting | bytes 131072
